TPU v7x, 256 devices: a whole 4x4x8 slice. The times are simulated.
256 devices in a mesh: gx: 8 (over x, core), gy: 4 (over y), gz: 8 (over z).
Axes of the slice: x: 4, y: 4, z: 8, core: 2. Of those that a mesh axis runs over, the one named last changes fastest.
Arguments:
- right_side: float32 [3, 64, 32, 64, 128], P(None, 'gx', 'gy', 'gz'), may hold values from -24 to 24
- stiffness: float32 [3, 64, 32, 64], P(None, 'gx', 'gy', 'gz'), may hold values from 0.25 to 4
- local_factor: bfloat16 [8, 4, 8, 2048, 2048], P('gx', 'gy', 'gz'), as said below
- basis: bfloat16 [8, 4, 8, 64, 1536], P('gx', 'gy', 'gz'), may hold values from -0.3125 to 0.3125
- coarse_map: int32 [8, 4, 8, 64], P('gx', 'gy', 'gz'), may hold values from 0 to 63, each once within a row
- margin_index: int32 [8, 4, 8, 512], P('gx', 'gy', 'gz'), may hold values from 0 to 1151, as said below
- coarse_inverse: bfloat16 [16384, 16384], P(('gx', 'gy', 'gz')), as said below
Outputs:
- solution: float32 [3, 64, 32, 64, 128], P(None, 'gx', 'gy', 'gz')
- residual_ratio: float32 [128], replicated
Inputs may be any that keep to these rules, and one draw needn't show every extreme that they name: `local_factor`: each subdomain's factor is zero above its diagonal. coarse_inverse is symmetric. `margin_index`: within each subdomain the 512 entries are distinct and increasing. `coarse_map`: each subdomain's entries are a permutation of 0 to 63.
All inputs are finite; a program needn't handle non-finite values.
Results may differ from a plain program's by a relative error of at most 0.0055.
Values may be sent and summed in bfloat16 or wider, within the bound.
No kernel may reach another device: no remote copies, remote signals or barrier semaphores. Data moves between devices by JAX's collectives and lax.ppermute only.
A program may use at most 64 MiB of HBM per device.

v0:
```python
import functools

import jax
import jax.numpy as jnp
from jax import lax
from jax.sharding import Mesh
from jax.sharding import PartitionSpec as P

GX_GY_GZ = ("gx_0", "gx_1", "gy", "gz")
GX = ("gx_0", "gx_1")


EPSILON = 1e-06


def one_axis_at_a_time(value, axes):
    return functools.reduce(lax.psum, axes, value)


def extended_2(value, sides, width):
    edges = {}
    for axis, dim in sides:
        peers, length = (lax.axis_size(axis), value.shape[dim])
        up = [(i, (i + 1) % peers) for i in range(peers - 1)]
        last = lax.slice_in_dim(value, length - width, length, axis=dim)
        leading = lax.slice_in_dim(value, 0, width, axis=dim)
        edges[dim] = (
            lax.ppermute(last, axis, up),
            lax.ppermute(leading, axis, [(b, a) for a, b in up]),
        )
    done = []
    for _, dim in sides:
        low, high = edges[dim]
        around = [(width, width) if d in done else (0, 0) for d in range(value.ndim)]
        value = jnp.concatenate([jnp.pad(low, around), value, jnp.pad(high, around)], axis=dim)
        done.append(dim)
    return value


def laid_out(parts, dim):
    parts = jnp.moveaxis(parts, 0, dim)
    shape = parts.shape
    return parts.reshape(*shape[:dim], shape[dim] * shape[dim + 1], *shape[dim + 2 :])


def gather_in_order(value, axes, order):
    parts = value
    for k in order:
        parts = lax.all_gather(parts, axes[k])
    done = order[::-1]
    back = [done.index(k) for k in range(len(axes))]
    parts = parts.transpose(*back, *range(len(axes), parts.ndim))
    return parts.reshape(-1, *value.shape)


def gathered_by_axis(value, axes, order, dim):
    return laid_out(gather_in_order(value, axes, order), dim)


def inner(left, right):
    return jnp.sum(left * right, axis=(0, 1, 2, 3))


def face_rows(padded):
    rhs_count = padded.shape[-1]
    slabs = [
        padded[:, 0, 1:-1, 1:-1],
        padded[:, -1, 1:-1, 1:-1],
        padded[:, 1:-1, 0, 1:-1],
        padded[:, 1:-1, -1, 1:-1],
        padded[:, 1:-1, 1:-1, 0],
        padded[:, 1:-1, 1:-1, -1],
    ]
    joined = jnp.concatenate([slab.reshape(slab.shape[0], -1, rhs_count) for slab in slabs], axis=1)
    return joined.reshape(-1, rhs_count)


def norm_sum(field):
    return one_axis_at_a_time(inner(field, field), GX_GY_GZ)


def orthogonalize(mapped, previous):
    partials = jnp.stack([inner(mapped, vector) for vector in previous] + [inner(mapped, mapped)])
    totals = one_axis_at_a_time(partials, GX_GY_GZ)
    coeffs = [totals[position] for position in range(len(previous))]
    remainder = mapped
    square = totals[-1]
    for weight_value, vector in zip(coeffs, previous):
        remainder = remainder - weight_value * vector
        square = square - weight_value * weight_value
    return (remainder, coeffs, jnp.sqrt(square + EPSILON))


def local(right_side, stiffness, local_factor, basis, coarse_map, margin_index, coarse_inverse):
    factor = local_factor.reshape(local_factor.shape[-2:])
    coarse_basis = basis.reshape(basis.shape[-2:])
    basis_count = coarse_basis.shape[0]
    coarse_ids = coarse_map.reshape(-1)
    margin_rows = margin_index.reshape(-1)
    placement_table = (
        coarse_ids[None, :] == lax.broadcasted_iota(jnp.int32, (basis_count, basis_count), 0)
    ).astype(jnp.float32)
    contract_first = (((0,), (0,)), ((), ()))

    def precondition(field):
        rounded = field.astype(jnp.bfloat16)
        padded = extended_2(rounded, ((GX, 1), ("gy", 2), ("gz", 3)), 1)
        own_rows = rounded.reshape(-1, rounded.shape[-1])
        extended = jnp.concatenate(
            [own_rows, jnp.take(face_rows(padded), margin_rows, axis=0)], axis=0
        )
        front_values = jnp.dot(factor, extended, preferred_element_type=jnp.float32).astype(
            jnp.bfloat16
        )
        back_sweep = lax.dot_general(
            factor, front_values, contract_first, preferred_element_type=jnp.float32
        )
        local_part = back_sweep[: own_rows.shape[0]]
        restricted = jnp.dot(coarse_basis, own_rows, preferred_element_type=jnp.float32)
        placed = jnp.dot(placement_table, restricted, precision=lax.Precision.HIGHEST).astype(
            jnp.bfloat16
        )
        solved = jnp.dot(
            coarse_inverse,
            gathered_by_axis(placed, GX_GY_GZ, (0, 2, 3, 1), 0),
            preferred_element_type=jnp.float32,
        )
        solved = solved.astype(jnp.bfloat16)
        own_coarse = lax.dot_general(
            placement_table,
            solved.astype(jnp.float32),
            contract_first,
            precision=lax.Precision.HIGHEST,
        ).astype(jnp.bfloat16)
        coarse_part = lax.dot_general(
            coarse_basis, own_coarse, contract_first, preferred_element_type=jnp.float32
        )
        return (local_part + coarse_part).reshape(field.shape)

    def operate(field):
        padded = extended_2(field.astype(jnp.bfloat16), ((GX, 1), ("gy", 2), ("gz", 3)), 1).astype(
            field.dtype
        )
        beside = padded[:, 2:, 1:-1, 1:-1] + padded[:, :-2, 1:-1, 1:-1]
        beside = beside + padded[:, 1:-1, 2:, 1:-1] + padded[:, 1:-1, :-2, 1:-1]
        beside = beside + padded[:, 1:-1, 1:-1, 2:] + padded[:, 1:-1, 1:-1, :-2]
        return (6.0 + stiffness[..., None]) * field - beside

    start_norm = jnp.sqrt(norm_sum(right_side) + EPSILON)
    basis_one = right_side / start_norm
    search_one = precondition(basis_one)
    remainder, first_coeffs, norm_two = orthogonalize(operate(search_one), [basis_one])
    basis_two = remainder / norm_two
    search_two = precondition(basis_two)
    remainder, second_coeffs, norm_three = orthogonalize(
        operate(search_two), [basis_one, basis_two]
    )
    along_one = first_coeffs[0]
    cross_two = second_coeffs[0]
    along_two = second_coeffs[1]
    radius_one = jnp.sqrt(along_one * along_one + norm_two * norm_two)
    cosine_one = along_one / radius_one
    sine_one = norm_two / radius_one
    turned_one = cosine_one * cross_two + sine_one * along_two
    turned_two = cosine_one * along_two - sine_one * cross_two
    radius_two = jnp.sqrt(turned_two * turned_two + norm_three * norm_three)
    cosine_two = turned_two / radius_two
    sine_two = norm_three / radius_two
    coef_two = -cosine_two * sine_one * start_norm / radius_two
    coef_one = (cosine_one * start_norm - turned_one * coef_two) / radius_one
    solution = coef_one * search_one + coef_two * search_two
    return (solution, sine_one * sine_two)


def solution(mesh):
    finer = Mesh(
        mesh.devices.reshape(4, 2, mesh.shape["gy"], mesh.shape["gz"]), ("gx_0", "gx_1", "gy", "gz")
    )
    placed = (
        P(None, GX, "gy", "gz", None),
        P(None, GX, "gy", "gz"),
        P(GX, "gy", "gz", None, None),
        P(GX, "gy", "gz", None, None),
        P(GX, "gy", "gz", None),
        P(GX, "gy", "gz", None),
        P(GX_GY_GZ, None),
    )
    return jax.shard_map(
        local,
        mesh=finer,
        in_specs=placed,
        out_specs=(P(None, GX, "gy", "gz", None), P()),
        check_vma=False,
    )
```

profile of v0, /device:TPU:8, one launch (start us, length us, event | category | flops | bytes accessed | tf_op | source)
XLA Modules:
  0.0 396.5 jit_solution(16053493213017205837)
XLA Ops:
  7.2 1.5 multiply_reduce_fusion.5
  8.7 10.5 %psum.84 = f32[128]{0:T(128)S(1)} all-reduce(f32[128]{0:T(128)S(1)} %multiply_reduce_fusion.5), channel_id=1, replica_groups=mesh['gx_0'=4,'gx_1'=2,'gy'=4,'gz'=8] {'gx_0'}, use_global_device_ids=true, to_apply=%region_1.0 | all-reduce | flops 128 | bytes 1024 | tf_op jit(solution)/shard_map/psum | solution.py:17
  19.2 2.5 psum.85
  21.7 8.7 %psum.86 = f32[128]{0:T(128)S(1)} all-reduce(f32[128]{0:T(128)S(1)} %psum.85), channel_id=1, replica_groups=mesh['gx_0'=4,'gx_1'=2,'gy'=4,'gz'=8] {'gy'}, use_global_device_ids=true, to_apply=%region_3.0 | all-reduce | flops 128 | bytes 1024 | tf_op jit(solution)/shard_map/psum | solution.py:17
  30.3 20.0 %psum.87 = f32[128]{0:T(128)S(1)} all-reduce(f32[128]{0:T(128)S(1)} %psum.86), channel_id=1, replica_groups=mesh['gx_0'=4,'gx_1'=2,'gy'=4,'gz'=8] {'gz'}, use_global_device_ids=true, to_apply=%region_4.0 | all-reduce | flops 128 | bytes 1024 | tf_op jit(solution)/shard_map/psum | solution.py:17
  50.3 1.2 fusion.93
  51.6 1.1 fusion.67
  52.9 11.9 %all-gather = bf16[256,128]{1,0:T(8,128)(2,1)S(1)} all-gather(bf16[64,128]{1,0:T(8,128)(2,1)S(1)} %convolution_convert_fusion.3), channel_id=2, replica_groups=mesh['gx_0'=4,'gx_1'=2,'gy'=4,'gz'=8] {'gx_0'}, dimensions={0}, use_global_device_ids=true | all-gather | bytes 81920 | tf_op jit(solution)/shard_map/all_gather | solution.py:49
  64.7 12.3 %all-gather.1 = bf16[16,64,128]{2,1,0:T(8,128)(2,1)} all-gather(bf16[4,64,128]{2,1,0:T(8,128)(2,1)S(1)} %bitcast.203), channel_id=3, replica_groups=mesh['gx_0'=4,'gx_1'=2,'gy'=4,'gz'=8] {'gy'}, dimensions={0}, use_global_device_ids=true | all-gather | bytes 327680 | tf_op jit(solution)/shard_map/all_gather | solution.py:49
  77.1 38.5 %all-gather.13.cloned.1.call-done = bf16[32,4,64,128]{3,2,1,0:T(8,128)(2,1)} async-done(((bf16[4,4,64,128]{3,2,1,0:T(8,128)(2,1)}), bf16[32,4,64,128]{3,2,1,0:T(8,128)(2,1)}) %all-gather.13.cloned.1.call-update) | async-done | bytes 2097168 | tf_op jit(solution)/shard_map/all_gather | solution.py:49
  115.7 1.3 collective-permute-start
  117.0 1.3 collective-permute-start.1
  118.3 3.4 collective-permute-start.2
  121.7 2.4 collective-permute-start.3
  124.3 3.2 collective-permute-start.4
  127.6 1.3 collective-permute-start.5
  129.7 4.4 %collective-permute-done.5 = bf16[3,8,8,1,128]{4,3,2,1,0:T(2,128)(2,1)S(1)} collective-permute-done((bf16[3,8,8,1,128]{4,3,2,1,0:T(2,128)(2,1)S(1)}, bf16[3,8,8,1,128]{4,3,2,1,0:T(2,128)(2,1)S(1)}, u32[]{:S(2)}, u32[]{:S(2)}) %collective-permute-start.5) | collective-permute-done | bytes 49184 | tf_op jit(solution)/shard_map/ppermute | solution.py:29
  134.1 1.3 gather_fusion
  135.6 10.8 %fusion.12 = f32[2048,128]{0,1:T(8,128)} fusion(bf16[1,1,1,2048,2048]{4,3,2,1,0:T(8,128)(2,1)} %param.11, bf16[512,128]{1,0:T(8,128)(2,1)S(1)} %broadcast_select_fusion.1, bf16[1536,128]{1,0:T(8,128)(2,1)S(1)} %bitcast.193), kind=kOutput, calls=%fused_computation.16 | convolution fusion | flops 2148794368 | bytes 9961472 | tf_op jit(solution)/shard_map/dot_general | solution.py:115
  146.4 3.1 copy.31
  149.6 0.9 convolution_convert_fusion.5
  151.1 1.1 copy.32
  152.3 1.3 convert_element_type.72
  153.8 1.3 collective-permute-start.11
  155.1 1.9 collective-permute-start.10
  157.0 3.9 collective-permute-start.7
  160.9 4.6 %collective-permute-start.6 = (bf16[3,8,8,1,128]{4,3,2,1,0:T(2,128)(2,1)S(1)}, bf16[3,8,8,1,128]{4,3,2,1,0:T(2,128)(2,1)S(1)}, u32[]{:S(2)}, u32[]{:S(2)}) collective-permute-start(bf16[3,8,8,1,128]{4,3,2,1,0:T(2,128)(2,1)S(1)} %get-tuple-element.29), channel_id=1, source_target_pairs={{0,1},{1,2},{2,3},{3,4},{4,5},{5,6},{6,7},{8,9},{9,10},{10,11},{11... | collective-permute-start | bytes 147464 | tf_op jit(solution)/shard_map/ppermute | solution.py:28
  165.5 1.3 collective-permute-start.9
  166.8 3.0 collective-permute-start.8
  171.5 1.5 multiply_reduce_fusion.4
  172.9 15.5 %psum.88 = f32[2,128]{1,0:T(2,128)S(1)} all-reduce(f32[2,128]{1,0:T(2,128)S(1)} %pad_maximum_fusion.1), channel_id=1, replica_groups=mesh['gx_0'=4,'gx_1'=2,'gy'=4,'gz'=8] {'gx_0'}, use_global_device_ids=true, to_apply=%region_7.9 | all-reduce | flops 256 | bytes 2048 | tf_op jit(solution)/shard_map/psum | solution.py:17
  188.4 2.5 psum.89
  190.9 8.6 %psum.90 = f32[2,128]{1,0:T(2,128)S(1)} all-reduce(f32[2,128]{1,0:T(2,128)S(1)} %psum.89), channel_id=1, replica_groups=mesh['gx_0'=4,'gx_1'=2,'gy'=4,'gz'=8] {'gy'}, use_global_device_ids=true, to_apply=%region_9.11 | all-reduce | flops 256 | bytes 2048 | tf_op jit(solution)/shard_map/psum | solution.py:17
  199.5 16.7 %psum.91 = f32[2,128]{1,0:T(2,128)S(1)} all-reduce(f32[2,128]{1,0:T(2,128)S(1)} %psum.90), channel_id=1, replica_groups=mesh['gx_0'=4,'gx_1'=2,'gy'=4,'gz'=8] {'gz'}, use_global_device_ids=true, to_apply=%region_10.12 | all-reduce | flops 256 | bytes 2048 | tf_op jit(solution)/shard_map/psum | solution.py:17
  216.2 1.3 fusion.92
  217.9 11.9 %all-gather.4 = bf16[256,128]{1,0:T(8,128)(2,1)S(1)} all-gather(bf16[64,128]{1,0:T(8,128)(2,1)S(1)} %convolution_convert_fusion.1), channel_id=6, replica_groups=mesh['gx_0'=4,'gx_1'=2,'gy'=4,'gz'=8] {'gx_0'}, dimensions={0}, use_global_device_ids=true | all-gather | bytes 81920 | tf_op jit(solution)/shard_map/all_gather | solution.py:49
  229.7 11.8 %all-gather.5 = bf16[16,64,128]{2,1,0:T(8,128)(2,1)} all-gather(bf16[4,64,128]{2,1,0:T(8,128)(2,1)S(1)} %bitcast.204), channel_id=7, replica_groups=mesh['gx_0'=4,'gx_1'=2,'gy'=4,'gz'=8] {'gy'}, dimensions={0}, use_global_device_ids=true | all-gather | bytes 327680 | tf_op jit(solution)/shard_map/all_gather | solution.py:49
  241.6 40.1 %all-gather.17.cloned.1.call-done = bf16[32,4,64,128]{3,2,1,0:T(8,128)(2,1)} async-done(((bf16[4,4,64,128]{3,2,1,0:T(8,128)(2,1)}), bf16[32,4,64,128]{3,2,1,0:T(8,128)(2,1)}) %all-gather.17.cloned.1.call-update) | async-done | bytes 2097168 | tf_op jit(solution)/shard_map/all_gather | solution.py:49
  281.7 1.3 collective-permute-start.12
  283.1 1.3 collective-permute-start.13
  284.4 3.4 collective-permute-start.14
  287.8 2.4 collective-permute-start.15
  290.3 3.2 collective-permute-start.16
  293.5 1.5 collective-permute-start.17
  298.2 1.9 collective-permute-done.17
  300.7 2.7 gather_fusion.1
  303.4 1.7 broadcast_select_fusion
  305.1 10.8 %fusion.15 = f32[2048,128]{0,1:T(8,128)} fusion(bf16[1,1,1,2048,2048]{4,3,2,1,0:T(8,128)(2,1)} %param.11, bf16[512,128]{1,0:T(8,128)(2,1)} %broadcast_select_fusion, bf16[1536,128]{1,0:T(8,128)(2,1)S(1)} %bitcast.195), kind=kOutput, calls=%fused_computation.17 | convolution fusion | flops 2148794368 | bytes 9961472 | tf_op jit(solution)/shard_map/dot_general | solution.py:115
  315.9 3.1 copy.33
  319.1 0.9 convolution_convert_fusion.4
  320.3 1.2 fusion.18
  321.5 2.3 copy.34
  323.8 1.3 convert_element_type.79
  325.3 1.3 collective-permute-start.23
  326.6 1.9 collective-permute-start.22
  328.5 3.9 collective-permute-start.19
  332.5 4.6 %collective-permute-start.18 = (bf16[3,8,8,1,128]{4,3,2,1,0:T(2,128)(2,1)S(1)}, bf16[3,8,8,1,128]{4,3,2,1,0:T(2,128)(2,1)S(1)}, u32[]{:S(2)}, u32[]{:S(2)}) collective-permute-start(bf16[3,8,8,1,128]{4,3,2,1,0:T(2,128)(2,1)S(1)} %get-tuple-element.17), channel_id=1, source_target_pairs={{0,1},{1,2},{2,3},{3,4},{4,5},{5,6},{6,7},{8,9},{9,10},{10,11},{11... | collective-permute-start | bytes 147464 | tf_op jit(solution)/shard_map/ppermute | solution.py:28
  337.0 1.3 collective-permute-start.21
  338.3 3.0 collective-permute-start.20
  343.7 15.5 %psum.92 = f32[3,128]{1,0:T(4,128)S(1)} all-reduce(f32[3,128]{1,0:T(4,128)S(1)} %pad_maximum_fusion), channel_id=1, replica_groups=mesh['gx_0'=4,'gx_1'=2,'gy'=4,'gz'=8] {'gx_0'}, use_global_device_ids=true, to_apply=%region_14.16 | all-reduce | flops 384 | bytes 3072 | tf_op jit(solution)/shard_map/psum | solution.py:17
  359.2 2.5 psum.93
  361.7 8.6 %psum.94 = f32[3,128]{1,0:T(4,128)S(1)} all-reduce(f32[3,128]{1,0:T(4,128)S(1)} %psum.93), channel_id=1, replica_groups=mesh['gx_0'=4,'gx_1'=2,'gy'=4,'gz'=8] {'gy'}, use_global_device_ids=true, to_apply=%region_16.18 | all-reduce | flops 384 | bytes 3072 | tf_op jit(solution)/shard_map/psum | solution.py:17
  370.3 16.7 %psum.95 = f32[3,128]{1,0:T(4,128)S(1)} all-reduce(f32[3,128]{1,0:T(4,128)S(1)} %psum.94), channel_id=1, replica_groups=mesh['gx_0'=4,'gx_1'=2,'gy'=4,'gz'=8] {'gz'}, use_global_device_ids=true, to_apply=%region_17.19 | all-reduce | flops 384 | bytes 3072 | tf_op jit(solution)/shard_map/psum | solution.py:17
  387.6 2.4 multiply_add_fusion
  (103 shorter events, 11.6 us)
Async XLA Ops:
  7.2 142.4 %copy-start = (bf16[64,16384]{1,0:T(8,128)(2,1)S(1)}, bf16[64,16384]{1,0:T(8,128)(2,1)}, u32[]{:S(2)}) copy-start(bf16[64,16384]{1,0:T(8,128)(2,1)} %param.15) | copy-start | bytes 6291460
  7.2 45.5 %copy-start.11 = (s32[1,1,1,64]{3,2,1,0:T(1,128)S(1)}, s32[1,1,1,64]{3,2,1,0:T(1,128)}, u32[]{:S(2)}) copy-start(s32[1,1,1,64]{3,2,1,0:T(1,128)} %param.13) | copy-start | bytes 772
  7.2 108.4 %all-gather.13.cloned.1.call-start = ((), (), s32[]{:S(2)}) async-start(), calls=%async_computation | async-start | bytes 2359296 | tf_op jit(solution)/shard_map/all_gather | solution.py:49
  50.3 77.2 %copy-start.12 = (s32[1,1,1,512]{3,2,1,0:T(1,128)S(1)}, s32[1,1,1,512]{3,2,1,0:T(1,128)}, u32[]{:S(2)}) copy-start(s32[1,1,1,512]{3,2,1,0:T(1,128)} %param.14) | copy-start | bytes 6148
  77.0 69.4 %all-gather.15.cloned.1.call-start = ((), (), s32[]{:S(2)}) async-start(), calls=%async_computation.1 | async-start | bytes 6291456 | tf_op jit(solution)/shard_map/all_gather | solution.py:49
  115.6 166.0 %all-gather.17.cloned.1.call-start = ((), (), s32[]{:S(2)}) async-start(), calls=%async_computation.2 | async-start | bytes 2359296 | tf_op jit(solution)/shard_map/all_gather | solution.py:49
  115.7 11.9 %collective-permute-start = (bf16[3,1,8,8,128]{4,3,2,1,0:T(8,128)(2,1)S(1)}, bf16[3,1,8,8,128]{4,3,2,1,0:T(8,128)(2,1)S(1)}, u32[]{:S(2)}, u32[]{:S(2)}) collective-permute-start(bf16[3,1,8,8,128]{4,3,2,1,0:T(8,128)(2,1)S(1)} %get-tuple-element.38), channel_id=1, source_target_pairs={{0,32},{32,64},{64,96},{96,128},{128,160},{160,192},{192,224},{1,3... | collective-permute-start | bytes 147464 | tf_op jit(solution)/shard_map/ppermute | solution.py:28
  117.0 11.9 %collective-permute-start.1 = (bf16[3,1,8,8,128]{4,3,2,1,0:T(8,128)(2,1)S(1)}, bf16[3,1,8,8,128]{4,3,2,1,0:T(8,128)(2,1)S(1)}, u32[]{:S(2)}, u32[]{:S(2)}) collective-permute-start(bf16[3,1,8,8,128]{4,3,2,1,0:T(8,128)(2,1)S(1)} %get-tuple-element.37), channel_id=1, source_target_pairs={{32,0},{64,32},{96,64},{128,96},{160,128},{192,160},{224,192},{33,... | collective-permute-start | bytes 147464 | tf_op jit(solution)/shard_map/ppermute | solution.py:29
  118.3 10.6 %collective-permute-start.2 = (bf16[3,8,1,8,128]{4,3,2,1,0:T(8,128)(2,1)S(1)}, bf16[3,8,1,8,128]{4,3,2,1,0:T(8,128)(2,1)S(1)}, u32[]{:S(2)}, u32[]{:S(2)}) collective-permute-start(bf16[3,8,1,8,128]{4,3,2,1,0:T(8,128)(2,1)S(1)} %get-tuple-element.36), channel_id=1, source_target_pairs={{0,8},{8,16},{16,24},{1,9},{9,17},{17,25},{2,10},{10,18},{18,26},{... | collective-permute-start | bytes 147464 | tf_op jit(solution)/shard_map/ppermute | solution.py:28
  121.7 7.2 %collective-permute-start.3 = (bf16[3,8,1,8,128]{4,3,2,1,0:T(8,128)(2,1)S(1)}, bf16[3,8,1,8,128]{4,3,2,1,0:T(8,128)(2,1)S(1)}, u32[]{:S(2)}, u32[]{:S(2)}) collective-permute-start(bf16[3,8,1,8,128]{4,3,2,1,0:T(8,128)(2,1)S(1)} %get-tuple-element.35), channel_id=1, source_target_pairs={{8,0},{16,8},{24,16},{9,1},{17,9},{25,17},{10,2},{18,10},{26,18},{... | collective-permute-start | bytes 147464 | tf_op jit(solution)/shard_map/ppermute | solution.py:29
  124.3 5.4 %collective-permute-start.4 = (bf16[3,8,8,1,128]{4,3,2,1,0:T(2,128)(2,1)S(1)}, bf16[3,8,8,1,128]{4,3,2,1,0:T(2,128)(2,1)S(1)}, u32[]{:S(2)}, u32[]{:S(2)}) collective-permute-start(bf16[3,8,8,1,128]{4,3,2,1,0:T(2,128)(2,1)S(1)} %get-tuple-element.34), channel_id=1, source_target_pairs={{0,1},{1,2},{2,3},{3,4},{4,5},{5,6},{6,7},{8,9},{9,10},{10,11},{11... | collective-permute-start | bytes 147464 | tf_op jit(solution)/shard_map/ppermute | solution.py:28
  127.6 6.5 %collective-permute-start.5 = (bf16[3,8,8,1,128]{4,3,2,1,0:T(2,128)(2,1)S(1)}, bf16[3,8,8,1,128]{4,3,2,1,0:T(2,128)(2,1)S(1)}, u32[]{:S(2)}, u32[]{:S(2)}) collective-permute-start(bf16[3,8,8,1,128]{4,3,2,1,0:T(2,128)(2,1)S(1)} %get-tuple-element.33), channel_id=1, source_target_pairs={{1,0},{2,1},{3,2},{4,3},{5,4},{6,5},{7,6},{9,8},{10,9},{11,10},{12... | collective-permute-start | bytes 147464 | tf_op jit(solution)/shard_map/ppermute | solution.py:29
  149.6 1.2 copy-start.5
  149.6 1.2 copy-start.7
  150.8 19.0 %copy-start.10 = (f32[3,8,8,8]{3,2,1,0:T(8,128)S(1)}, f32[3,8,8,8]{3,2,1,0:T(8,128)}, u32[]{:S(2)}) copy-start(f32[3,8,8,8]{3,2,1,0:T(8,128)} %param.10) | copy-start | bytes 18436
  152.3 19.2 %copy-start.1 = (f32[3,8,8,8,128]{4,3,2,1,0:T(8,128)S(1)}, f32[3,8,8,8,128]{4,3,2,1,0:T(8,128)}, u32[]{:S(2)}) copy-start(f32[3,8,8,8,128]{4,3,2,1,0:T(8,128)} %param.9) | copy-start | bytes 2359300
  152.3 19.2 %copy-start.2 = (f32[1536,128]{1,0:T(8,128)S(1)}, f32[1536,128]{1,0:T(8,128)}, u32[]{:S(2)}) copy-start(f32[1536,128]{1,0:T(8,128)} %copy.32) | copy-start | bytes 2359300
  153.8 13.0 %collective-permute-start.11 = (bf16[3,8,8,1,128]{4,3,2,1,0:T(2,128)(2,1)S(1)}, bf16[3,8,8,1,128]{4,3,2,1,0:T(2,128)(2,1)S(1)}, u32[]{:S(2)}, u32[]{:S(2)}) collective-permute-start(bf16[3,8,8,1,128]{4,3,2,1,0:T(2,128)(2,1)S(1)} %get-tuple-element.30), channel_id=1, source_target_pairs={{1,0},{2,1},{3,2},{4,3},{5,4},{6,5},{7,6},{9,8},{10,9},{11,10},{12... | collective-permute-start | bytes 147464 | tf_op jit(solution)/shard_map/ppermute | solution.py:29
  155.1 14.8 %collective-permute-start.10 = (bf16[3,8,1,8,128]{4,3,2,1,0:T(8,128)(2,1)S(1)}, bf16[3,8,1,8,128]{4,3,2,1,0:T(8,128)(2,1)S(1)}, u32[]{:S(2)}, u32[]{:S(2)}) collective-permute-start(bf16[3,8,1,8,128]{4,3,2,1,0:T(8,128)(2,1)S(1)} %get-tuple-element.32), channel_id=1, source_target_pairs={{8,0},{16,8},{24,16},{9,1},{17,9},{25,17},{10,2},{18,10},{26,18},{... | collective-permute-start | bytes 147464 | tf_op jit(solution)/shard_map/ppermute | solution.py:29
  157.0 12.9 %collective-permute-start.7 = (bf16[3,8,1,8,128]{4,3,2,1,0:T(8,128)(2,1)S(1)}, bf16[3,8,1,8,128]{4,3,2,1,0:T(8,128)(2,1)S(1)}, u32[]{:S(2)}, u32[]{:S(2)}) collective-permute-start(bf16[3,8,1,8,128]{4,3,2,1,0:T(8,128)(2,1)S(1)} %get-tuple-element.31), channel_id=1, source_target_pairs={{0,8},{8,16},{16,24},{1,9},{9,17},{17,25},{2,10},{10,18},{18,26},{... | collective-permute-start | bytes 147464 | tf_op jit(solution)/shard_map/ppermute | solution.py:28
  160.9 9.0 %collective-permute-start.6 = (bf16[3,8,8,1,128]{4,3,2,1,0:T(2,128)(2,1)S(1)}, bf16[3,8,8,1,128]{4,3,2,1,0:T(2,128)(2,1)S(1)}, u32[]{:S(2)}, u32[]{:S(2)}) collective-permute-start(bf16[3,8,8,1,128]{4,3,2,1,0:T(2,128)(2,1)S(1)} %get-tuple-element.29), channel_id=1, source_target_pairs={{0,1},{1,2},{2,3},{3,4},{4,5},{5,6},{6,7},{8,9},{9,10},{10,11},{11... | collective-permute-start | bytes 147464 | tf_op jit(solution)/shard_map/ppermute | solution.py:28
  165.5 4.4 %collective-permute-start.9 = (bf16[3,1,8,8,128]{4,3,2,1,0:T(8,128)(2,1)S(1)}, bf16[3,1,8,8,128]{4,3,2,1,0:T(8,128)(2,1)S(1)}, u32[]{:S(2)}, u32[]{:S(2)}) collective-permute-start(bf16[3,1,8,8,128]{4,3,2,1,0:T(8,128)(2,1)S(1)} %get-tuple-element.28), channel_id=1, source_target_pairs={{32,0},{64,32},{96,64},{128,96},{160,128},{192,160},{224,192},{33,... | collective-permute-start | bytes 147464 | tf_op jit(solution)/shard_map/ppermute | solution.py:29
  166.8 3.9 collective-permute-start.8
  169.9 3.1 copy-start.8
  241.5 74.4 %all-gather.19.cloned.1.call-start = ((), (), s32[]{:S(2)}) async-start(), calls=%async_computation.3 | async-start | bytes 6291456 | tf_op jit(solution)/shard_map/all_gather | solution.py:49
  281.7 11.8 %collective-permute-start.12 = (bf16[3,1,8,8,128]{4,3,2,1,0:T(8,128)(2,1)S(1)}, bf16[3,1,8,8,128]{4,3,2,1,0:T(8,128)(2,1)S(1)}, u32[]{:S(2)}, u32[]{:S(2)}) collective-permute-start(bf16[3,1,8,8,128]{4,3,2,1,0:T(8,128)(2,1)S(1)} %get-tuple-element.26), channel_id=1, source_target_pairs={{0,32},{32,64},{64,96},{96,128},{128,160},{160,192},{192,224},{1,3... | collective-permute-start | bytes 147464 | tf_op jit(solution)/shard_map/ppermute | solution.py:28
  283.1 12.5 %collective-permute-start.13 = (bf16[3,1,8,8,128]{4,3,2,1,0:T(8,128)(2,1)S(1)}, bf16[3,1,8,8,128]{4,3,2,1,0:T(8,128)(2,1)S(1)}, u32[]{:S(2)}, u32[]{:S(2)}) collective-permute-start(bf16[3,1,8,8,128]{4,3,2,1,0:T(8,128)(2,1)S(1)} %get-tuple-element.25), channel_id=1, source_target_pairs={{32,0},{64,32},{96,64},{128,96},{160,128},{192,160},{224,192},{33,... | collective-permute-start | bytes 147464 | tf_op jit(solution)/shard_map/ppermute | solution.py:29
  284.4 11.8 %collective-permute-start.14 = (bf16[3,8,1,8,128]{4,3,2,1,0:T(8,128)(2,1)S(1)}, bf16[3,8,1,8,128]{4,3,2,1,0:T(8,128)(2,1)S(1)}, u32[]{:S(2)}, u32[]{:S(2)}) collective-permute-start(bf16[3,8,1,8,128]{4,3,2,1,0:T(8,128)(2,1)S(1)} %get-tuple-element.24), channel_id=1, source_target_pairs={{0,8},{8,16},{16,24},{1,9},{9,17},{17,25},{2,10},{10,18},{18,26},{... | collective-permute-start | bytes 147464 | tf_op jit(solution)/shard_map/ppermute | solution.py:28
  287.8 9.1 %collective-permute-start.15 = (bf16[3,8,1,8,128]{4,3,2,1,0:T(8,128)(2,1)S(1)}, bf16[3,8,1,8,128]{4,3,2,1,0:T(8,128)(2,1)S(1)}, u32[]{:S(2)}, u32[]{:S(2)}) collective-permute-start(bf16[3,8,1,8,128]{4,3,2,1,0:T(8,128)(2,1)S(1)} %get-tuple-element.23), channel_id=1, source_target_pairs={{8,0},{16,8},{24,16},{9,1},{17,9},{25,17},{10,2},{18,10},{26,18},{... | collective-permute-start | bytes 147464 | tf_op jit(solution)/shard_map/ppermute | solution.py:29
  290.3 7.3 %collective-permute-start.16 = (bf16[3,8,8,1,128]{4,3,2,1,0:T(2,128)(2,1)S(1)}, bf16[3,8,8,1,128]{4,3,2,1,0:T(2,128)(2,1)S(1)}, u32[]{:S(2)}, u32[]{:S(2)}) collective-permute-start(bf16[3,8,8,1,128]{4,3,2,1,0:T(2,128)(2,1)S(1)} %get-tuple-element.22), channel_id=1, source_target_pairs={{0,1},{1,2},{2,3},{3,4},{4,5},{5,6},{6,7},{8,9},{9,10},{10,11},{11... | collective-permute-start | bytes 147464 | tf_op jit(solution)/shard_map/ppermute | solution.py:28
  293.5 6.5 %collective-permute-start.17 = (bf16[3,8,8,1,128]{4,3,2,1,0:T(2,128)(2,1)S(1)}, bf16[3,8,8,1,128]{4,3,2,1,0:T(2,128)(2,1)S(1)}, u32[]{:S(2)}, u32[]{:S(2)}) collective-permute-start(bf16[3,8,8,1,128]{4,3,2,1,0:T(2,128)(2,1)S(1)} %get-tuple-element.21), channel_id=1, source_target_pairs={{1,0},{2,1},{3,2},{4,3},{5,4},{6,5},{7,6},{9,8},{10,9},{11,10},{12... | collective-permute-start | bytes 147464 | tf_op jit(solution)/shard_map/ppermute | solution.py:29
  319.1 1.2 copy-start.6
  323.8 19.2 %copy-start.3 = (f32[1536,128]{1,0:T(8,128)S(1)}, f32[1536,128]{1,0:T(8,128)}, u32[]{:S(2)}) copy-start(f32[1536,128]{1,0:T(8,128)} %copy.34) | copy-start | bytes 2359300
  323.8 19.2 %copy-start.4 = (f32[3,8,8,8,128]{4,3,2,1,0:T(8,128)S(1)}, f32[3,8,8,8,128]{4,3,2,1,0:T(8,128)}, u32[]{:S(2)}) copy-start(f32[3,8,8,8,128]{4,3,2,1,0:T(8,128)} %get-tuple-element.14) | copy-start | bytes 2359300
  323.8 19.2 %copy-start.9 = (f32[3,8,8,8]{3,2,1,0:T(8,128)S(1)}, f32[3,8,8,8]{3,2,1,0:T(8,128)}, u32[]{:S(2)}) copy-start(f32[3,8,8,8]{3,2,1,0:T(8,128)} %copy-done.8) | copy-start | bytes 18436
  325.3 13.0 %collective-permute-start.23 = (bf16[3,8,8,1,128]{4,3,2,1,0:T(2,128)(2,1)S(1)}, bf16[3,8,8,1,128]{4,3,2,1,0:T(2,128)(2,1)S(1)}, u32[]{:S(2)}, u32[]{:S(2)}) collective-permute-start(bf16[3,8,8,1,128]{4,3,2,1,0:T(2,128)(2,1)S(1)} %get-tuple-element.18), channel_id=1, source_target_pairs={{1,0},{2,1},{3,2},{4,3},{5,4},{6,5},{7,6},{9,8},{10,9},{11,10},{12... | collective-permute-start | bytes 147464 | tf_op jit(solution)/shard_map/ppermute | solution.py:29
  326.6 14.8 %collective-permute-start.22 = (bf16[3,8,1,8,128]{4,3,2,1,0:T(8,128)(2,1)S(1)}, bf16[3,8,1,8,128]{4,3,2,1,0:T(8,128)(2,1)S(1)}, u32[]{:S(2)}, u32[]{:S(2)}) collective-permute-start(bf16[3,8,1,8,128]{4,3,2,1,0:T(8,128)(2,1)S(1)} %get-tuple-element.20), channel_id=1, source_target_pairs={{8,0},{16,8},{24,16},{9,1},{17,9},{25,17},{10,2},{18,10},{26,18},{... | collective-permute-start | bytes 147464 | tf_op jit(solution)/shard_map/ppermute | solution.py:29
  328.5 12.9 %collective-permute-start.19 = (bf16[3,8,1,8,128]{4,3,2,1,0:T(8,128)(2,1)S(1)}, bf16[3,8,1,8,128]{4,3,2,1,0:T(8,128)(2,1)S(1)}, u32[]{:S(2)}, u32[]{:S(2)}) collective-permute-start(bf16[3,8,1,8,128]{4,3,2,1,0:T(8,128)(2,1)S(1)} %get-tuple-element.19), channel_id=1, source_target_pairs={{0,8},{8,16},{16,24},{1,9},{9,17},{17,25},{2,10},{10,18},{18,26},{... | collective-permute-start | bytes 147464 | tf_op jit(solution)/shard_map/ppermute | solution.py:28
  332.5 8.9 %collective-permute-start.18 = (bf16[3,8,8,1,128]{4,3,2,1,0:T(2,128)(2,1)S(1)}, bf16[3,8,8,1,128]{4,3,2,1,0:T(2,128)(2,1)S(1)}, u32[]{:S(2)}, u32[]{:S(2)}) collective-permute-start(bf16[3,8,8,1,128]{4,3,2,1,0:T(2,128)(2,1)S(1)} %get-tuple-element.17), channel_id=1, source_target_pairs={{0,1},{1,2},{2,3},{3,4},{4,5},{5,6},{6,7},{8,9},{9,10},{10,11},{11... | collective-permute-start | bytes 147464 | tf_op jit(solution)/shard_map/ppermute | solution.py:28
  337.0 4.4 %collective-permute-start.21 = (bf16[3,1,8,8,128]{4,3,2,1,0:T(8,128)(2,1)S(1)}, bf16[3,1,8,8,128]{4,3,2,1,0:T(8,128)(2,1)S(1)}, u32[]{:S(2)}, u32[]{:S(2)}) collective-permute-start(bf16[3,1,8,8,128]{4,3,2,1,0:T(8,128)(2,1)S(1)} %get-tuple-element.16), channel_id=1, source_target_pairs={{32,0},{64,32},{96,64},{128,96},{160,128},{192,160},{224,192},{33,... | collective-permute-start | bytes 147464 | tf_op jit(solution)/shard_map/ppermute | solution.py:29
  338.3 3.9 collective-permute-start.20
Sparse Core Ops, SparseCore 0:
  77.1 38.3 all-gather.12
  117.4 17.5 all-gather.14
  241.6 39.9 all-gather.16
  283.3 17.5 all-gather.18
where the time goes:
time: 398 us; the launch traced here: 397 us
  blocking collectives  176 us (44%)
  waiting for transfers between devices  87.3 us (22%)
  starting transfers between devices  58.2 us (15%)
  matrix products  26.9 us (7%)
  local copies, waits for them, and re-layouts  18.6 us (5%)
  other arithmetic  15.2 us (4%)
  between operations  14.5 us (4%)
    psum x12, blocking collectives, one_axis_at_a_time(): return functools.reduce(lax.psum, axes, value)  128 us
    all_gather x4, waiting for transfers between devices, gather_in_order(): parts = lax.all_gather(parts, axes[k])  78.5 us
    all_gather x4, blocking collectives, gather_in_order(): parts = lax.all_gather(parts, axes[k])  47.8 us
    ppermute x12, starting transfers between devices, extended_2(): lax.ppermute(last, axis, up)  38.8 us
    dot_general x2, matrix products, precondition(): lax.dot_general(factor, front_values, contract_first, preferred_element_t...  21.7 us
    ppermute x12, starting transfers between devices, extended_2(): lax.ppermute(leading, axis, [(b, a) for a, b in up])  19.3 us
  transfers between devices with their start and end apart: 28, of which 7 were waited for; matrix products, arithmetic and copies ran while one was open for 8% of the time, Pallas kernels for 0%

commit v1 on v0

--- a/solution.py
+++ b/solution.py
@@ -1,5 +1,3 @@
-import functools
-
 import jax
 import jax.numpy as jnp
 from jax import lax
@@ -11,10 +9,7 @@
 
 
 EPSILON = 1e-06
-
-
-def one_axis_at_a_time(value, axes):
-    return functools.reduce(lax.psum, axes, value)
+SCALE = 2.0**-14
 
 
 def extended_2(value, sides, width):
@@ -37,26 +32,6 @@
     return value
 
 
-def laid_out(parts, dim):
-    parts = jnp.moveaxis(parts, 0, dim)
-    shape = parts.shape
-    return parts.reshape(*shape[:dim], shape[dim] * shape[dim + 1], *shape[dim + 2 :])
-
-
-def gather_in_order(value, axes, order):
-    parts = value
-    for k in order:
-        parts = lax.all_gather(parts, axes[k])
-    done = order[::-1]
-    back = [done.index(k) for k in range(len(axes))]
-    parts = parts.transpose(*back, *range(len(axes), parts.ndim))
-    return parts.reshape(-1, *value.shape)
-
-
-def gathered_by_axis(value, axes, order, dim):
-    return laid_out(gather_in_order(value, axes, order), dim)
-
-
 def inner(left, right):
     return jnp.sum(left * right, axis=(0, 1, 2, 3))
 
@@ -75,20 +50,46 @@
     return joined.reshape(-1, rhs_count)
 
 
-def norm_sum(field):
-    return one_axis_at_a_time(inner(field, field), GX_GY_GZ)
-
-
-def orthogonalize(mapped, previous):
-    partials = jnp.stack([inner(mapped, vector) for vector in previous] + [inner(mapped, mapped)])
-    totals = one_axis_at_a_time(partials, GX_GY_GZ)
-    coeffs = [totals[position] for position in range(len(previous))]
-    remainder = mapped
-    square = totals[-1]
-    for weight_value, vector in zip(coeffs, previous):
-        remainder = remainder - weight_value * vector
-        square = square - weight_value * weight_value
-    return (remainder, coeffs, jnp.sqrt(square + EPSILON))
+def weights(gram):
+    raw_raw, one_raw, one_one, two_raw, two_one, two_two = (gram[i] for i in range(6))
+    start_square = raw_raw / (SCALE * SCALE) + EPSILON
+    start_norm = jnp.sqrt(start_square)
+    size = start_norm * SCALE
+    square = size * size
+    kept = raw_raw / square
+    along_one = one_raw / square
+    rest_one = one_one / square - along_one * along_one * (2.0 - kept)
+    rest_one = jnp.maximum(rest_one, 0.0) + EPSILON
+    norm_two = jnp.sqrt(rest_one)
+    kept_two = (rest_one - EPSILON) / rest_one
+    shared = along_one * (1.0 - kept) / norm_two
+    cross_two = (two_raw - along_one * one_raw) / (square * norm_two)
+    along_two = (
+        (two_one - along_one * two_raw) - along_one * (one_one - along_one * one_raw)
+    ) / (square * rest_one)
+    image_square = (two_two - along_one * (2.0 * two_one - along_one * one_one)) / (
+        square * rest_one
+    )
+    rest_two = (
+        image_square
+        - cross_two * cross_two * (2.0 - kept)
+        - along_two * along_two * (2.0 - kept_two)
+        + 2.0 * cross_two * along_two * shared
+    )
+    norm_three = jnp.sqrt(jnp.maximum(rest_two, 0.0) + EPSILON)
+    radius_one = jnp.sqrt(along_one * along_one + norm_two * norm_two)
+    cosine_one = along_one / radius_one
+    sine_one = norm_two / radius_one
+    turned_one = cosine_one * cross_two + sine_one * along_two
+    turned_two = cosine_one * along_two - sine_one * cross_two
+    radius_two = jnp.sqrt(turned_two * turned_two + norm_three * norm_three)
+    cosine_two = turned_two / radius_two
+    sine_two = norm_three / radius_two
+    coef_two = -cosine_two * sine_one * start_norm / radius_two
+    coef_one = (cosine_one * start_norm - turned_one * coef_two) / radius_one
+    weight_two = coef_two / (size * norm_two)
+    weight_one = coef_one / size - along_one * weight_two
+    return (weight_one, weight_two, sine_one * sine_two)
 
 
 def local(right_side, stiffness, local_factor, basis, coarse_map, margin_index, coarse_inverse):
@@ -122,7 +123,7 @@
         )
         solved = jnp.dot(
             coarse_inverse,
-            gathered_by_axis(placed, GX_GY_GZ, (0, 2, 3, 1), 0),
+            lax.all_gather(placed, GX_GY_GZ, tiled=True),
             preferred_element_type=jnp.float32,
         )
         solved = solved.astype(jnp.bfloat16)
@@ -146,30 +147,26 @@
         beside = beside + padded[:, 1:-1, 1:-1, 2:] + padded[:, 1:-1, 1:-1, :-2]
         return (6.0 + stiffness[..., None]) * field - beside
 
-    start_norm = jnp.sqrt(norm_sum(right_side) + EPSILON)
-    basis_one = right_side / start_norm
-    search_one = precondition(basis_one)
-    remainder, first_coeffs, norm_two = orthogonalize(operate(search_one), [basis_one])
-    basis_two = remainder / norm_two
-    search_two = precondition(basis_two)
-    remainder, second_coeffs, norm_three = orthogonalize(
-        operate(search_two), [basis_one, basis_two]
+    raw = right_side * SCALE
+    search_one = precondition(raw)
+    image_one = operate(search_one)
+    search_two = precondition(image_one)
+    image_two = operate(search_two)
+    gram = lax.psum(
+        jnp.stack(
+            [
+                inner(raw, raw),
+                inner(image_one, raw),
+                inner(image_one, image_one),
+                inner(image_two, raw),
+                inner(image_two, image_one),
+                inner(image_two, image_two),
+            ]
+        ),
+        GX_GY_GZ,
     )
-    along_one = first_coeffs[0]
-    cross_two = second_coeffs[0]
-    along_two = second_coeffs[1]
-    radius_one = jnp.sqrt(along_one * along_one + norm_two * norm_two)
-    cosine_one = along_one / radius_one
-    sine_one = norm_two / radius_one
-    turned_one = cosine_one * cross_two + sine_one * along_two
-    turned_two = cosine_one * along_two - sine_one * cross_two
-    radius_two = jnp.sqrt(turned_two * turned_two + norm_three * norm_three)
-    cosine_two = turned_two / radius_two
-    sine_two = norm_three / radius_two
-    coef_two = -cosine_two * sine_one * start_norm / radius_two
-    coef_one = (cosine_one * start_norm - turned_one * coef_two) / radius_one
-    solution = coef_one * search_one + coef_two * search_two
-    return (solution, sine_one * sine_two)
+    weight_one, weight_two, ratio = weights(gram)
+    return (weight_one * search_one + weight_two * search_two, ratio)
 
 
 def solution(mesh):

time: 398 us -> 392 us (0.985)
  blocking collectives: 176 us -> 75.9 us
  waiting for transfers between devices: 87.3 us -> 184 us
  matrix products: 26.9 us -> 34.2 us
  local copies, waits for them, and re-layouts: 18.6 us -> 12.3 us
  other arithmetic: 15.2 us -> 11 us
    all_gather x4 -> x2, waiting for transfers between devices: 78.5 us -> 171 us  [precondition(): lax.all_gather(placed, GX_GY_GZ, tiled=True)]
    psum x12 -> x1, blocking collectives: 128 us -> 75.9 us  [local(): lax.psum(jnp.stack([inner(raw, raw), inner(image_one, raw), inner(image_o...]
    all_gather x4 -> x0, blocking collectives: 47.8 us -> none  [gather_in_order(): parts = lax.all_gather(parts, axes[k])]
    transpose x2 -> x0, local copies, waits for them, and re-layouts: 6.29 us -> none  [gather_in_order(): parts = parts.transpose(*back, *range(len(axes), parts.ndim))]
    dot_general x2, matrix products: 1.76 us -> 6.23 us  [precondition(): jnp.dot(coarse_inverse, lax.all_gather(placed, GX_GY_GZ, tiled=True), pre...]
  transfers between devices with their start and end apart: 28 -> 26, of which waited for: 7 -> 9; matrix products, arithmetic and copies ran while one was open for 8% -> 8% of each run, Pallas kernels for 0% -> 0%
where the time goes in v1:
time: 392 us; the launch traced here: 390 us
  waiting for transfers between devices  184 us (47%)
  blocking collectives  75.9 us (19%)
  starting transfers between devices  57.1 us (15%)
  matrix products  34.2 us (9%)
  between operations  14.7 us (4%)
  local copies, waits for them, and re-layouts  12.3 us (3%)
  other arithmetic  11 us (3%)
    all_gather x2, waiting for transfers between devices, precondition(): lax.all_gather(placed, GX_GY_GZ, tiled=True)  171 us
    psum x1, blocking collectives, local(): lax.psum(jnp.stack([inner(raw, raw), inner(image_one, raw), inner(image_o...  75.9 us
    ppermute x12, starting transfers between devices, extended_2(): lax.ppermute(last, axis, up)  36.4 us
    dot_general x2, matrix products, precondition(): lax.dot_general(factor, front_values, contract_first, preferred_element_t...  21.7 us
    ppermute x12, starting transfers between devices, extended_2(): lax.ppermute(leading, axis, [(b, a) for a, b in up])  20.7 us
    ppermute x12, waiting for transfers between devices, extended_2(): lax.ppermute(leading, axis, [(b, a) for a, b in up])  8.9 us
  transfers between devices with their start and end apart: 26, of which 9 were waited for; matrix products, arithmetic and copies ran while one was open for 8% of the time, Pallas kernels for 0%

profile of v1, /device:TPU:8, one launch (start us, length us, event | category | flops | bytes accessed | tf_op | source)
XLA Modules:
  0.0 389.7 jit_solution(13444253315848552626)
XLA Ops:
  7.2 1.4 multiply_convert_fusion
  8.6 1.1 fusion.67
  9.7 1.4 convolution_convert_fusion.3
  11.2 1.3 collective-permute-start.1
  12.5 3.0 collective-permute-start
  15.6 4.1 %collective-permute-start.3 = (bf16[3,8,1,8,128]{4,3,2,1,0:T(8,128)(2,1)S(1)}, bf16[3,8,1,8,128]{4,3,2,1,0:T(8,128)(2,1)S(1)}, u32[]{:S(2)}, u32[]{:S(2)}) collective-permute-start(bf16[3,8,1,8,128]{4,3,2,1,0:T(8,128)(2,1)S(1)} %get-tuple-element.41), channel_id=1, source_target_pairs={{8,0},{16,8},{24,16},{9,1},{17,9},{25,17},{10,2},{18,10},{26,18},{... | collective-permute-start | bytes 147464 | tf_op jit(solution)/shard_map/ppermute | solution.py:24
  19.7 1.9 collective-permute-start.2
  21.7 1.3 collective-permute-start.5
  23.1 4.6 %collective-permute-start.4 = (bf16[3,8,8,1,128]{4,3,2,1,0:T(2,128)(2,1)S(1)}, bf16[3,8,8,1,128]{4,3,2,1,0:T(2,128)(2,1)S(1)}, u32[]{:S(2)}, u32[]{:S(2)}) collective-permute-start(bf16[3,8,8,1,128]{4,3,2,1,0:T(2,128)(2,1)S(1)} %get-tuple-element.40), channel_id=1, source_target_pairs={{0,1},{1,2},{2,3},{3,4},{4,5},{5,6},{6,7},{8,9},{9,10},{10,11},{11... | collective-permute-start | bytes 147464 | tf_op jit(solution)/shard_map/ppermute | solution.py:23
  27.8 2.5 collective-permute-done.4
  30.3 1.3 gather_fusion
  31.8 10.9 %fusion.12 = f32[2048,128]{0,1:T(8,128)} fusion(bf16[1,1,1,2048,2048]{4,3,2,1,0:T(8,128)(2,1)} %param.11, bf16[512,128]{1,0:T(8,128)(2,1)S(1)} %broadcast_select_fusion.1, bf16[1536,128]{1,0:T(8,128)(2,1)S(1)} %bitcast.199), kind=kOutput, calls=%fused_computation.16 | convolution fusion | flops 2148794368 | bytes 9961472 | tf_op jit(solution)/shard_map/dot_general | solution.py:116
  42.6 88.4 %all-gather.3.cloned.1.call-done = bf16[16384,128]{1,0:T(8,128)(2,1)} async-done(((bf16[64,128]{1,0:T(8,128)(2,1)}), bf16[16384,128]{1,0:T(8,128)(2,1)}) %all-gather.3.cloned.1.call-update) | async-done | bytes 4194320 | tf_op jit(solution)/shard_map/all_gather | solution.py:126
  131.1 3.1 convolution_convert_fusion.5
  134.2 0.2 convolution_convert_fusion.2
  134.4 1.2 fusion.19
  135.6 1.4 copy.27
  137.2 2.1 collective-permute-start.8
  139.4 1.3 collective-permute-start.9
  140.7 3.7 collective-permute-start.7
  144.4 2.2 collective-permute-start.10
  146.6 2.6 collective-permute-start.6
  149.2 1.3 collective-permute-start.11
  150.5 0.2 collective-permute-done.10
  150.8 1.2 collective-permute-done.6
  151.9 4.2 %collective-permute-done.11 = bf16[3,8,8,1,128]{4,3,2,1,0:T(2,128)(2,1)S(1)} collective-permute-done((bf16[3,8,8,1,128]{4,3,2,1,0:T(2,128)(2,1)S(1)}, bf16[3,8,8,1,128]{4,3,2,1,0:T(2,128)(2,1)S(1)}, u32[]{:S(2)}, u32[]{:S(2)}) %collective-permute-start.11) | collective-permute-done | bytes 49184 | tf_op jit(solution)/shard_map/ppermute | solution.py:24
  156.1 0.7 fusion.40
  156.9 1.4 fusion.97
  158.2 0.2 fusion.70
  158.4 0.8 convolution_convert_fusion.1
  159.2 1.4 collective-permute-start.12
  160.8 1.3 collective-permute-start.13
  162.1 1.9 collective-permute-start.15
  164.0 3.9 %collective-permute-start.14 = (bf16[3,8,1,8,128]{4,3,2,1,0:T(8,128)(2,1)S(1)}, bf16[3,8,1,8,128]{4,3,2,1,0:T(8,128)(2,1)S(1)}, u32[]{:S(2)}, u32[]{:S(2)}) collective-permute-start(bf16[3,8,1,8,128]{4,3,2,1,0:T(8,128)(2,1)S(1)} %get-tuple-element.30), channel_id=1, source_target_pairs={{0,8},{8,16},{16,24},{1,9},{9,17},{17,25},{2,10},{10,18},{18,26},{... | collective-permute-start | bytes 147464 | tf_op jit(solution)/shard_map/ppermute | solution.py:23
  168.0 1.3 collective-permute-start.17
  169.3 4.7 %collective-permute-start.16 = (bf16[3,8,8,1,128]{4,3,2,1,0:T(2,128)(2,1)S(1)}, bf16[3,8,8,1,128]{4,3,2,1,0:T(2,128)(2,1)S(1)}, u32[]{:S(2)}, u32[]{:S(2)}) collective-permute-start(bf16[3,8,8,1,128]{4,3,2,1,0:T(2,128)(2,1)S(1)} %get-tuple-element.28), channel_id=1, source_target_pairs={{0,1},{1,2},{2,3},{3,4},{4,5},{5,6},{6,7},{8,9},{9,10},{10,11},{11... | collective-permute-start | bytes 147464 | tf_op jit(solution)/shard_map/ppermute | solution.py:23
  174.0 0.6 bitcast_dynamic-update-slice_fusion.7
  174.7 0.6 bitcast_dynamic-update-slice_fusion.6
  175.3 0.6 bitcast_dynamic-update-slice_fusion.5
  175.9 0.6 bitcast_dynamic-update-slice_fusion.4
  176.6 0.6 bitcast_dynamic-update-slice_fusion.1
  177.2 0.6 bitcast_dynamic-update-slice_fusion
  177.8 2.7 gather_fusion.1
  180.5 1.7 broadcast_select_fusion
  182.2 10.9 %fusion.15 = f32[2048,128]{0,1:T(8,128)} fusion(bf16[1,1,1,2048,2048]{4,3,2,1,0:T(8,128)(2,1)} %param.11, bf16[512,128]{1,0:T(8,128)(2,1)} %broadcast_select_fusion, bf16[1536,128]{1,0:T(8,128)(2,1)S(1)} %bitcast.197), kind=kOutput, calls=%fused_computation.17 | convolution fusion | flops 2148794368 | bytes 9961472 | tf_op jit(solution)/shard_map/dot_general | solution.py:116
  193.1 82.3 %all-gather.5.cloned.1.call-done = bf16[16384,128]{1,0:T(8,128)(2,1)} async-done(((bf16[64,128]{1,0:T(8,128)(2,1)}), bf16[16384,128]{1,0:T(8,128)(2,1)}) %all-gather.5.cloned.1.call-update) | async-done | bytes 4194320 | tf_op jit(solution)/shard_map/all_gather | solution.py:126
  275.4 3.1 convolution_convert_fusion.4
  278.7 1.2 fusion.18
  279.9 2.3 copy.28
  282.2 1.3 convert_element_type.79
  283.7 2.1 collective-permute-start.20
  285.9 1.3 collective-permute-start.21
  287.2 3.7 collective-permute-start.19
  290.8 2.2 collective-permute-start.22
  293.0 2.6 collective-permute-start.18
  295.7 1.3 collective-permute-start.23
  297.0 0.3 collective-permute-done.22
  297.2 1.2 collective-permute-done.18
  298.4 4.2 %collective-permute-done.23 = bf16[3,8,8,1,128]{4,3,2,1,0:T(2,128)(2,1)S(1)} collective-permute-done((bf16[3,8,8,1,128]{4,3,2,1,0:T(2,128)(2,1)S(1)}, bf16[3,8,8,1,128]{4,3,2,1,0:T(2,128)(2,1)S(1)}, u32[]{:S(2)}, u32[]{:S(2)}) %collective-permute-start.23) | collective-permute-done | bytes 49184 | tf_op jit(solution)/shard_map/ppermute | solution.py:24
  302.6 0.7 fusion.43
  303.4 0.8 multiply_reduce_fusion
  304.2 75.9 %psum.7 = f32[6,128]{1,0:T(8,128)S(1)} all-reduce(f32[6,128]{1,0:T(8,128)S(1)} %stack.27), channel_id=1, replica_groups=mesh['gx_0'=4,'gx_1'=2,'gy'=4,'gz'=8] {'gx_0','gx_1','gy','gz'}, use_global_device_ids=true, to_apply=%region_6.8 | all-reduce | flops 768 | bytes 6144 | tf_op jit(solution)/shard_map/psum | solution.py:155
  380.0 0.6 multiply_multiply_fusion
  380.6 2.2 multiply_add_fusion
  (72 shorter events, 1.4 us)
Async XLA Ops:
  7.2 123.9 %copy-start = (bf16[64,16384]{1,0:T(8,128)(2,1)S(1)}, bf16[64,16384]{1,0:T(8,128)(2,1)}, u32[]{:S(2)}) copy-start(bf16[64,16384]{1,0:T(8,128)(2,1)} %param.15) | copy-start | bytes 6291460
  7.2 15.9 %copy-start.11 = (s32[1,1,1,512]{3,2,1,0:T(1,128)S(1)}, s32[1,1,1,512]{3,2,1,0:T(1,128)}, u32[]{:S(2)}) copy-start(s32[1,1,1,512]{3,2,1,0:T(1,128)} %param.14) | copy-start | bytes 6148
  7.2 123.9 %all-gather.3.cloned.1.call-start = ((), (), s32[]{:S(2)}) async-start(), calls=%async_computation | async-start | bytes 4210688 | tf_op jit(solution)/shard_map/all_gather | solution.py:126
  11.2 264.2 %all-gather.5.cloned.1.call-start = ((), (), s32[]{:S(2)}) async-start(), calls=%async_computation.1 | async-start | bytes 4210688 | tf_op jit(solution)/shard_map/all_gather | solution.py:126
  11.2 16.4 %collective-permute-start.1 = (bf16[3,1,8,8,128]{4,3,2,1,0:T(8,128)(2,1)S(1)}, bf16[3,1,8,8,128]{4,3,2,1,0:T(8,128)(2,1)S(1)}, u32[]{:S(2)}, u32[]{:S(2)}) collective-permute-start(bf16[3,1,8,8,128]{4,3,2,1,0:T(8,128)(2,1)S(1)} %get-tuple-element.43), channel_id=1, source_target_pairs={{32,0},{64,32},{96,64},{128,96},{160,128},{192,160},{224,192},{33,... | collective-permute-start | bytes 147464 | tf_op jit(solution)/shard_map/ppermute | solution.py:24
  12.5 10.6 %collective-permute-start = (bf16[3,1,8,8,128]{4,3,2,1,0:T(8,128)(2,1)S(1)}, bf16[3,1,8,8,128]{4,3,2,1,0:T(8,128)(2,1)S(1)}, u32[]{:S(2)}, u32[]{:S(2)}) collective-permute-start(bf16[3,1,8,8,128]{4,3,2,1,0:T(8,128)(2,1)S(1)} %get-tuple-element.44), channel_id=1, source_target_pairs={{0,32},{32,64},{64,96},{96,128},{128,160},{160,192},{192,224},{1,3... | collective-permute-start | bytes 147464 | tf_op jit(solution)/shard_map/ppermute | solution.py:23
  15.6 12.1 %collective-permute-start.3 = (bf16[3,8,1,8,128]{4,3,2,1,0:T(8,128)(2,1)S(1)}, bf16[3,8,1,8,128]{4,3,2,1,0:T(8,128)(2,1)S(1)}, u32[]{:S(2)}, u32[]{:S(2)}) collective-permute-start(bf16[3,8,1,8,128]{4,3,2,1,0:T(8,128)(2,1)S(1)} %get-tuple-element.41), channel_id=1, source_target_pairs={{8,0},{16,8},{24,16},{9,1},{17,9},{25,17},{10,2},{18,10},{26,18},{... | collective-permute-start | bytes 147464 | tf_op jit(solution)/shard_map/ppermute | solution.py:24
  19.7 8.0 %collective-permute-start.2 = (bf16[3,8,1,8,128]{4,3,2,1,0:T(8,128)(2,1)S(1)}, bf16[3,8,1,8,128]{4,3,2,1,0:T(8,128)(2,1)S(1)}, u32[]{:S(2)}, u32[]{:S(2)}) collective-permute-start(bf16[3,8,1,8,128]{4,3,2,1,0:T(8,128)(2,1)S(1)} %get-tuple-element.42), channel_id=1, source_target_pairs={{0,8},{8,16},{16,24},{1,9},{9,17},{17,25},{2,10},{10,18},{18,26},{... | collective-permute-start | bytes 147464 | tf_op jit(solution)/shard_map/ppermute | solution.py:23
  21.7 8.5 %collective-permute-start.5 = (bf16[3,8,8,1,128]{4,3,2,1,0:T(2,128)(2,1)S(1)}, bf16[3,8,8,1,128]{4,3,2,1,0:T(2,128)(2,1)S(1)}, u32[]{:S(2)}, u32[]{:S(2)}) collective-permute-start(bf16[3,8,8,1,128]{4,3,2,1,0:T(2,128)(2,1)S(1)} %get-tuple-element.39), channel_id=1, source_target_pairs={{1,0},{2,1},{3,2},{4,3},{5,4},{6,5},{7,6},{9,8},{10,9},{11,10},{12... | collective-permute-start | bytes 147464 | tf_op jit(solution)/shard_map/ppermute | solution.py:24
  23.1 7.1 %collective-permute-start.4 = (bf16[3,8,8,1,128]{4,3,2,1,0:T(2,128)(2,1)S(1)}, bf16[3,8,8,1,128]{4,3,2,1,0:T(2,128)(2,1)S(1)}, u32[]{:S(2)}, u32[]{:S(2)}) collective-permute-start(bf16[3,8,8,1,128]{4,3,2,1,0:T(2,128)(2,1)S(1)} %get-tuple-element.40), channel_id=1, source_target_pairs={{0,1},{1,2},{2,3},{3,4},{4,5},{5,6},{6,7},{8,9},{9,10},{10,11},{11... | collective-permute-start | bytes 147464 | tf_op jit(solution)/shard_map/ppermute | solution.py:23
  42.6 91.6 %copy-start.10 = (s32[1,1,1,64]{3,2,1,0:T(1,128)S(1)}, s32[1,1,1,64]{3,2,1,0:T(1,128)}, u32[]{:S(2)}) copy-start(s32[1,1,1,64]{3,2,1,0:T(1,128)} %param.13) | copy-start | bytes 772
  42.6 91.8 %copy-start.4 = (bf16[1,1,1,64,1536]{4,3,2,1,0:T(8,128)(2,1)S(1)}, bf16[1,1,1,64,1536]{4,3,2,1,0:T(8,128)(2,1)}, u32[]{:S(2)}) copy-start(bf16[1,1,1,64,1536]{4,3,2,1,0:T(8,128)(2,1)} %param.12) | copy-start | bytes 589828
  131.1 3.3 copy-start.2
  134.4 16.1 %copy-start.9 = (f32[3,8,8,8]{3,2,1,0:T(8,128)S(1)}, f32[3,8,8,8]{3,2,1,0:T(8,128)}, u32[]{:S(2)}) copy-start(f32[3,8,8,8]{3,2,1,0:T(8,128)} %param.10) | copy-start | bytes 18436
  137.2 11.9 %collective-permute-start.8 = (bf16[3,1,8,8,128]{4,3,2,1,0:T(8,128)(2,1)S(1)}, bf16[3,1,8,8,128]{4,3,2,1,0:T(8,128)(2,1)S(1)}, u32[]{:S(2)}, u32[]{:S(2)}) collective-permute-start(bf16[3,1,8,8,128]{4,3,2,1,0:T(8,128)(2,1)S(1)} %get-tuple-element.33), channel_id=1, source_target_pairs={{0,32},{32,64},{64,96},{96,128},{128,160},{160,192},{192,224},{1,3... | collective-permute-start | bytes 147464 | tf_op jit(solution)/shard_map/ppermute | solution.py:23
  139.4 11.1 %collective-permute-start.9 = (bf16[3,1,8,8,128]{4,3,2,1,0:T(8,128)(2,1)S(1)}, bf16[3,1,8,8,128]{4,3,2,1,0:T(8,128)(2,1)S(1)}, u32[]{:S(2)}, u32[]{:S(2)}) collective-permute-start(bf16[3,1,8,8,128]{4,3,2,1,0:T(8,128)(2,1)S(1)} %get-tuple-element.34), channel_id=1, source_target_pairs={{32,0},{64,32},{96,64},{128,96},{160,128},{192,160},{224,192},{33,... | collective-permute-start | bytes 147464 | tf_op jit(solution)/shard_map/ppermute | solution.py:24
  140.7 9.8 %collective-permute-start.7 = (bf16[3,8,1,8,128]{4,3,2,1,0:T(8,128)(2,1)S(1)}, bf16[3,8,1,8,128]{4,3,2,1,0:T(8,128)(2,1)S(1)}, u32[]{:S(2)}, u32[]{:S(2)}) collective-permute-start(bf16[3,8,1,8,128]{4,3,2,1,0:T(8,128)(2,1)S(1)} %get-tuple-element.37), channel_id=1, source_target_pairs={{0,8},{8,16},{16,24},{1,9},{9,17},{17,25},{2,10},{10,18},{18,26},{... | collective-permute-start | bytes 147464 | tf_op jit(solution)/shard_map/ppermute | solution.py:23
  144.4 6.4 %collective-permute-start.10 = (bf16[3,8,1,8,128]{4,3,2,1,0:T(8,128)(2,1)S(1)}, bf16[3,8,1,8,128]{4,3,2,1,0:T(8,128)(2,1)S(1)}, u32[]{:S(2)}, u32[]{:S(2)}) collective-permute-start(bf16[3,8,1,8,128]{4,3,2,1,0:T(8,128)(2,1)S(1)} %get-tuple-element.38), channel_id=1, source_target_pairs={{8,0},{16,8},{24,16},{9,1},{17,9},{25,17},{10,2},{18,10},{26,18},{... | collective-permute-start | bytes 147464 | tf_op jit(solution)/shard_map/ppermute | solution.py:24
  146.6 5.4 %collective-permute-start.6 = (bf16[3,8,8,1,128]{4,3,2,1,0:T(2,128)(2,1)S(1)}, bf16[3,8,8,1,128]{4,3,2,1,0:T(2,128)(2,1)S(1)}, u32[]{:S(2)}, u32[]{:S(2)}) collective-permute-start(bf16[3,8,8,1,128]{4,3,2,1,0:T(2,128)(2,1)S(1)} %get-tuple-element.35), channel_id=1, source_target_pairs={{0,1},{1,2},{2,3},{3,4},{4,5},{5,6},{6,7},{8,9},{9,10},{10,11},{11... | collective-permute-start | bytes 147464 | tf_op jit(solution)/shard_map/ppermute | solution.py:23
  149.2 6.9 %collective-permute-start.11 = (bf16[3,8,8,1,128]{4,3,2,1,0:T(2,128)(2,1)S(1)}, bf16[3,8,8,1,128]{4,3,2,1,0:T(2,128)(2,1)S(1)}, u32[]{:S(2)}, u32[]{:S(2)}) collective-permute-start(bf16[3,8,8,1,128]{4,3,2,1,0:T(2,128)(2,1)S(1)} %get-tuple-element.36), channel_id=1, source_target_pairs={{1,0},{2,1},{3,2},{4,3},{5,4},{6,5},{7,6},{9,8},{10,9},{11,10},{12... | collective-permute-start | bytes 147464 | tf_op jit(solution)/shard_map/ppermute | solution.py:24
  150.5 7.7 %copy-start.7 = (f32[3,8,8,8]{3,2,1,0:T(8,128)}, f32[3,8,8,8]{3,2,1,0:T(8,128)S(1)}, u32[]{:S(2)}) copy-start(f32[3,8,8,8]{3,2,1,0:T(8,128)S(1)} %broadcast_add_fusion) | copy-start | bytes 18436
  159.2 10.0 %collective-permute-start.12 = (bf16[3,1,8,8,128]{4,3,2,1,0:T(8,128)(2,1)S(1)}, bf16[3,1,8,8,128]{4,3,2,1,0:T(8,128)(2,1)S(1)}, u32[]{:S(2)}, u32[]{:S(2)}) collective-permute-start(bf16[3,1,8,8,128]{4,3,2,1,0:T(8,128)(2,1)S(1)} %get-tuple-element.32), channel_id=1, source_target_pairs={{0,32},{32,64},{64,96},{96,128},{128,160},{160,192},{192,224},{1,3... | collective-permute-start | bytes 147464 | tf_op jit(solution)/shard_map/ppermute | solution.py:23
  160.8 13.8 %collective-permute-start.13 = (bf16[3,1,8,8,128]{4,3,2,1,0:T(8,128)(2,1)S(1)}, bf16[3,1,8,8,128]{4,3,2,1,0:T(8,128)(2,1)S(1)}, u32[]{:S(2)}, u32[]{:S(2)}) collective-permute-start(bf16[3,1,8,8,128]{4,3,2,1,0:T(8,128)(2,1)S(1)} %get-tuple-element.31), channel_id=1, source_target_pairs={{32,0},{64,32},{96,64},{128,96},{160,128},{192,160},{224,192},{33,... | collective-permute-start | bytes 147464 | tf_op jit(solution)/shard_map/ppermute | solution.py:24
  162.1 13.8 %collective-permute-start.15 = (bf16[3,8,1,8,128]{4,3,2,1,0:T(8,128)(2,1)S(1)}, bf16[3,8,1,8,128]{4,3,2,1,0:T(8,128)(2,1)S(1)}, u32[]{:S(2)}, u32[]{:S(2)}) collective-permute-start(bf16[3,8,1,8,128]{4,3,2,1,0:T(8,128)(2,1)S(1)} %get-tuple-element.29), channel_id=1, source_target_pairs={{8,0},{16,8},{24,16},{9,1},{17,9},{25,17},{10,2},{18,10},{26,18},{... | collective-permute-start | bytes 147464 | tf_op jit(solution)/shard_map/ppermute | solution.py:24
  164.0 11.2 %collective-permute-start.14 = (bf16[3,8,1,8,128]{4,3,2,1,0:T(8,128)(2,1)S(1)}, bf16[3,8,1,8,128]{4,3,2,1,0:T(8,128)(2,1)S(1)}, u32[]{:S(2)}, u32[]{:S(2)}) collective-permute-start(bf16[3,8,1,8,128]{4,3,2,1,0:T(8,128)(2,1)S(1)} %get-tuple-element.30), channel_id=1, source_target_pairs={{0,8},{8,16},{16,24},{1,9},{9,17},{17,25},{2,10},{10,18},{18,26},{... | collective-permute-start | bytes 147464 | tf_op jit(solution)/shard_map/ppermute | solution.py:23
  168.0 9.2 %collective-permute-start.17 = (bf16[3,8,8,1,128]{4,3,2,1,0:T(2,128)(2,1)S(1)}, bf16[3,8,8,1,128]{4,3,2,1,0:T(2,128)(2,1)S(1)}, u32[]{:S(2)}, u32[]{:S(2)}) collective-permute-start(bf16[3,8,8,1,128]{4,3,2,1,0:T(2,128)(2,1)S(1)} %get-tuple-element.27), channel_id=1, source_target_pairs={{1,0},{2,1},{3,2},{4,3},{5,4},{6,5},{7,6},{9,8},{10,9},{11,10},{12... | collective-permute-start | bytes 147464 | tf_op jit(solution)/shard_map/ppermute | solution.py:24
  169.3 7.3 %collective-permute-start.16 = (bf16[3,8,8,1,128]{4,3,2,1,0:T(2,128)(2,1)S(1)}, bf16[3,8,8,1,128]{4,3,2,1,0:T(2,128)(2,1)S(1)}, u32[]{:S(2)}, u32[]{:S(2)}) collective-permute-start(bf16[3,8,8,1,128]{4,3,2,1,0:T(2,128)(2,1)S(1)} %get-tuple-element.28), channel_id=1, source_target_pairs={{0,1},{1,2},{2,3},{3,4},{4,5},{5,6},{6,7},{8,9},{9,10},{10,11},{11... | collective-permute-start | bytes 147464 | tf_op jit(solution)/shard_map/ppermute | solution.py:23
  275.4 3.3 copy-start.3
  282.2 21.2 %copy-start.1 = (f32[1536,128]{1,0:T(8,128)S(1)}, f32[1536,128]{1,0:T(8,128)}, u32[]{:S(2)}) copy-start(f32[1536,128]{1,0:T(8,128)} %copy.28) | copy-start | bytes 2359300
  282.2 21.2 %copy-start.5 = (f32[3,8,8,8,128]{4,3,2,1,0:T(8,128)S(1)}, f32[3,8,8,8,128]{4,3,2,1,0:T(8,128)}, u32[]{:S(2)}) copy-start(f32[3,8,8,8,128]{4,3,2,1,0:T(8,128)} %get-tuple-element.20) | copy-start | bytes 2359300
  282.2 21.2 %copy-start.6 = (f32[3,8,8,8,128]{4,3,2,1,0:T(8,128)S(1)}, f32[3,8,8,8,128]{4,3,2,1,0:T(8,128)}, u32[]{:S(2)}) copy-start(f32[3,8,8,8,128]{4,3,2,1,0:T(8,128)} %param.9) | copy-start | bytes 2359300
  282.2 21.2 %copy-start.8 = (f32[3,8,8,8]{3,2,1,0:T(8,128)S(1)}, f32[3,8,8,8]{3,2,1,0:T(8,128)}, u32[]{:S(2)}) copy-start(f32[3,8,8,8]{3,2,1,0:T(8,128)} %copy-done.7) | copy-start | bytes 18436
  283.7 11.9 %collective-permute-start.20 = (bf16[3,1,8,8,128]{4,3,2,1,0:T(8,128)(2,1)S(1)}, bf16[3,1,8,8,128]{4,3,2,1,0:T(8,128)(2,1)S(1)}, u32[]{:S(2)}, u32[]{:S(2)}) collective-permute-start(bf16[3,1,8,8,128]{4,3,2,1,0:T(8,128)(2,1)S(1)} %get-tuple-element.21), channel_id=1, source_target_pairs={{0,32},{32,64},{64,96},{96,128},{128,160},{160,192},{192,224},{1,3... | collective-permute-start | bytes 147464 | tf_op jit(solution)/shard_map/ppermute | solution.py:23
  285.9 11.1 %collective-permute-start.21 = (bf16[3,1,8,8,128]{4,3,2,1,0:T(8,128)(2,1)S(1)}, bf16[3,1,8,8,128]{4,3,2,1,0:T(8,128)(2,1)S(1)}, u32[]{:S(2)}, u32[]{:S(2)}) collective-permute-start(bf16[3,1,8,8,128]{4,3,2,1,0:T(8,128)(2,1)S(1)} %get-tuple-element.22), channel_id=1, source_target_pairs={{32,0},{64,32},{96,64},{128,96},{160,128},{192,160},{224,192},{33,... | collective-permute-start | bytes 147464 | tf_op jit(solution)/shard_map/ppermute | solution.py:24
  287.2 9.8 %collective-permute-start.19 = (bf16[3,8,1,8,128]{4,3,2,1,0:T(8,128)(2,1)S(1)}, bf16[3,8,1,8,128]{4,3,2,1,0:T(8,128)(2,1)S(1)}, u32[]{:S(2)}, u32[]{:S(2)}) collective-permute-start(bf16[3,8,1,8,128]{4,3,2,1,0:T(8,128)(2,1)S(1)} %get-tuple-element.25), channel_id=1, source_target_pairs={{0,8},{8,16},{16,24},{1,9},{9,17},{17,25},{2,10},{10,18},{18,26},{... | collective-permute-start | bytes 147464 | tf_op jit(solution)/shard_map/ppermute | solution.py:23
  290.8 6.4 %collective-permute-start.22 = (bf16[3,8,1,8,128]{4,3,2,1,0:T(8,128)(2,1)S(1)}, bf16[3,8,1,8,128]{4,3,2,1,0:T(8,128)(2,1)S(1)}, u32[]{:S(2)}, u32[]{:S(2)}) collective-permute-start(bf16[3,8,1,8,128]{4,3,2,1,0:T(8,128)(2,1)S(1)} %get-tuple-element.26), channel_id=1, source_target_pairs={{8,0},{16,8},{24,16},{9,1},{17,9},{25,17},{10,2},{18,10},{26,18},{... | collective-permute-start | bytes 147464 | tf_op jit(solution)/shard_map/ppermute | solution.py:24
  293.0 5.4 %collective-permute-start.18 = (bf16[3,8,8,1,128]{4,3,2,1,0:T(2,128)(2,1)S(1)}, bf16[3,8,8,1,128]{4,3,2,1,0:T(2,128)(2,1)S(1)}, u32[]{:S(2)}, u32[]{:S(2)}) collective-permute-start(bf16[3,8,8,1,128]{4,3,2,1,0:T(2,128)(2,1)S(1)} %get-tuple-element.23), channel_id=1, source_target_pairs={{0,1},{1,2},{2,3},{3,4},{4,5},{5,6},{6,7},{8,9},{9,10},{10,11},{11... | collective-permute-start | bytes 147464 | tf_op jit(solution)/shard_map/ppermute | solution.py:23
  295.7 7.0 %collective-permute-start.23 = (bf16[3,8,8,1,128]{4,3,2,1,0:T(2,128)(2,1)S(1)}, bf16[3,8,8,1,128]{4,3,2,1,0:T(2,128)(2,1)S(1)}, u32[]{:S(2)}, u32[]{:S(2)}) collective-permute-start(bf16[3,8,8,1,128]{4,3,2,1,0:T(2,128)(2,1)S(1)} %get-tuple-element.24), channel_id=1, source_target_pairs={{1,0},{2,1},{3,2},{4,3},{5,4},{6,5},{7,6},{9,8},{10,9},{11,10},{12... | collective-permute-start | bytes 147464 | tf_op jit(solution)/shard_map/ppermute | solution.py:24
Sparse Core Ops, SparseCore 0:
  12.4 118.6 all-gather.2
  159.3 115.9 all-gather.4
